TPU v7x, 32 devices: a whole 2x2x4 slice. The times are simulated.
32 devices in a mesh: seq: 8 (over y, x, core), head: 4 (over z).
Axes of the slice: x: 2, y: 2, z: 4, core: 2. Of those that a mesh axis runs over, the one named last changes fastest.
Arguments:
- queries: bfloat16 [256, 128, 576], P('seq', 'head'), may hold values from -1024 to 1024
- latents: bfloat16 [1024, 576], P('seq'), may hold values from -6 to 6
- out_grad: bfloat16 [256, 128, 512], P('seq', 'head'), may hold values from -6 to 6
- layer_out: bfloat16 [256, 128, 512], P('seq', 'head'), may hold values from -4 to 4
- query_start: int32 [8], P('seq'), may hold values from 0 to 1023, as said below
Outputs:
- query_grad: bfloat16 [256, 128, 576], P('seq', 'head')
- latent_grad: float32 [1024, 576], P(('seq', 'head'))
Inputs may be any that keep to these rules, and one draw needn't show every extreme that they name: Shard i holds the 32 queries at consecutive positions from query_start[i]; queries past the last latent position see every latent row.
All inputs are finite; a program needn't handle non-finite values.
Results may differ from a plain program's by a relative error of at most 0.0049.
Values may be sent and summed in bfloat16 or wider, within the bound.
A program may use at most 64 MiB of HBM per device.

v0:
```python
import jax
import jax.numpy as jnp
from jax import lax
from jax.sharding import PartitionSpec as P

score_scale = 192 ** (-0.5)
masked_score = -1e30


def shifted(block, axis, distance):
    devices = range(lax.axis_size(axis))
    route = [((i - distance) % len(devices), i) for i in devices]
    return lax.ppermute(block, axis, route)


def visible_mask(first_key, key_rows, query_pos):
    key_pos = first_key + lax.iota(jnp.int32, key_rows)
    return key_pos[:, None] <= query_pos[None, :]


def score_block(block_rows, query_rows):
    return (
        lax.dot_general(
            block_rows, query_rows, (((1,), (1,)), ((), ())), preferred_element_type=jnp.float32
        )
        * score_scale
    )


def norm_step(running, block_rows, first_row, query_rows, query_pos):
    run_max, run_sum = running
    shown = visible_mask(first_row, block_rows.shape[0], query_pos)
    scores = jnp.where(shown, score_block(block_rows, query_rows), masked_score)
    new_max = jnp.maximum(run_max, jnp.max(scores, axis=0))
    weights = jnp.where(shown, jnp.exp(scores - new_max[None, :]), 0.0)
    run_sum = jnp.sum(weights, axis=0)
    return (new_max, run_sum)


def grad_block(block_rows, first_row, query_rows, grad_rows, row_delta, log_norm, query_pos):
    shown = visible_mask(first_row, block_rows.shape[0], query_pos)
    scores = score_block(block_rows, query_rows)
    weights = jnp.where(
        shown, jnp.exp(jnp.where(shown, scores - log_norm[None, :], masked_score)), 0.0
    )
    value_width = grad_rows.shape[1]
    prob_grad = lax.dot_general(
        block_rows[:, :value_width],
        grad_rows,
        (((1,), (1,)), ((), ())),
        preferred_element_type=jnp.float32,
    )
    dscore = (score_scale * weights * (prob_grad - row_delta[None, :])).astype(jnp.bfloat16)
    key_term = jnp.dot(dscore, query_rows, preferred_element_type=jnp.float32)
    value_term = jnp.dot(
        weights.astype(jnp.bfloat16), grad_rows, preferred_element_type=jnp.float32
    )
    key_term = key_term + jnp.pad(value_term, ((0, 0), (0, block_rows.shape[1] - value_width)))
    query_term = lax.dot_general(
        dscore, block_rows, (((0,), (0,)), ((), ())), preferred_element_type=jnp.float32
    )
    return (key_term, query_term)


def per_device(queries, latents, out_grad, layer_out, query_start):
    query_count, head_count, key_width = queries.shape
    row_count = query_count * head_count
    query_rows = queries.reshape(row_count, key_width)
    grad_rows = out_grad.reshape(row_count, out_grad.shape[2])
    row_delta = jnp.sum(
        out_grad.astype(jnp.float32) * layer_out.astype(jnp.float32), axis=2
    ).reshape(row_count)
    query_pos = query_start[0] + lax.iota(jnp.int32, row_count) // head_count
    key_count = latents.shape[0]
    cycle_size = lax.axis_size("seq")
    my_index = lax.axis_index("seq")
    start_state = (
        jnp.full((row_count,), masked_score, jnp.float32),
        jnp.zeros((row_count,), jnp.float32),
    )
    block_rows = lax.all_gather(latents, "seq", axis=0, tiled=True)
    running = start_state
    running = norm_step(running, block_rows, jnp.int32(0), query_rows, query_pos)
    add_stored = block_rows
    (run_max, run_sum), stored = (running, add_stored)
    log_norm = run_max + jnp.log(run_sum)

    def visit(first_row, rows, grad_sum, query_sum):
        block_rows = lax.dynamic_slice_in_dim(stored, first_row, rows, 0)
        key_term, query_term = grad_block(
            block_rows, first_row, query_rows, grad_rows, row_delta, log_norm, query_pos
        )
        return (grad_sum + key_term, query_sum + query_term)

    query_start_sum = jnp.zeros((row_count, key_width), jnp.float32)

    def cycle_turn(turn_index, state):
        grad_sum, query_sum = state
        owner_index = (my_index - turn_index - 1) % cycle_size
        grad_sum, query_sum = visit(owner_index * key_count, key_count, grad_sum, query_sum)
        return (shifted(grad_sum, "seq", 1), query_sum)

    start_sum = jnp.zeros((key_count, key_width), jnp.float32)
    grad_sum, query_sum = lax.fori_loop(0, cycle_size - 1, cycle_turn, (start_sum, query_start_sum))
    owned_sum, query_sum = visit(my_index * key_count, key_count, grad_sum, query_sum)
    latent_grad = lax.psum_scatter(owned_sum, "head", scatter_dimension=0, tiled=True)
    query_grad = query_sum.astype(jnp.bfloat16).reshape(query_count, head_count, key_width)
    return (query_grad, latent_grad)


def solution(mesh):
    placed = (
        P("seq", "head", None),
        P("seq", None),
        P("seq", "head", None),
        P("seq", "head", None),
        P("seq"),
    )
    return jax.shard_map(
        per_device,
        mesh=mesh,
        in_specs=placed,
        out_specs=(P("seq", "head", None), P(("seq", "head"), None)),
        check_vma=False,
    )
```

profile of v0, /device:TPU:0, one launch (start us, length us, event | category | flops | bytes accessed | tf_op | source)
XLA Modules:
  0.0 184.6 jit_solution(665887214875149356)
XLA Ops:
  7.2 1.7 copy.12
  9.0 1.9 %multiply_reduce_fusion = f32[32,32]{1,0:T(8,128)S(1)} fusion(bf16[32,32,512]{2,1,0:T(8,128)(2,1)} %param.10, bf16[32,32,512]{2,1,0:T(8,128)(2,1)} %param.9), kind=kLoop, calls=%fused_computation.34 | loop fusion | flops 2096128 | bytes 2101248 | tf_op jit(solution)/shard_map/reduce_sum | solution.py:70
  11.7 25.9 %all-gather.2.cloned.1.call-done = bf16[1024,576]{1,0:T(8,128)(2,1)} async-done(((bf16[128,576]{1,0:T(8,128)(2,1)}), bf16[1024,576]{1,0:T(8,128)(2,1)}) %all-gather.2.cloned.1.call-update) | async-done | bytes 1179664 | tf_op jit(solution)/shard_map/all_gather | solution.py:81
  37.7 3.6 %fusion.21 = (f32[1024]{0:T(1024)S(1)}, f32[1024,1024]{1,0:T(8,128)S(1)}) fusion(s32[1024]{0:T(1024)S(1)} %fusion.34, bf16[1024,576]{1,0:T(8,128)(2,1)} %all-gather.2.cloned.1.call-done, bf16[1024,576]{1,0:T(8,128)(2,1)} %bitcast.39), kind=kOutput, calls=%fused_computation.32 | convolution fusion | flops 1212152832 | bytes 6561792 | tf_op jit(solution)/shard_map/dot_general | solution.py:23
  41.3 1.2 select_reduce_fusion
  42.6 1.6 fusion.25
  44.3 0.8 copy-done.6
  45.0 1.0 fusion.29
  46.1 0.7 broadcast_in_dim.58
  46.8 104.9 %while.19 = (s32[]{:T(128)}, f32[128,576]{0,1:T(8,128)}, f32[1024,576]{0,1:T(8,128)S(1)}, s32[]{:T(128)}, bf16[1024,576]{1,0:T(8,128)(2,1)}, /*index=5*/bf16[102...) while((s32[]{:T(128)}, f32[128,576]{0,1:T(8,128)}, ...), condition=%wide.wide.region_4.5_spmd.clone, body=%wide.wide.region_3.4_spmd.clone.sunk | while | flops 724067456 | bytes 20202964 | solution.py:104
  47.5 2.0 %fusion.96 = f32[128,1024]{1,0:T(8,128)S(1)} fusion(bf16[1024,576]{1,0:T(8,128)(2,1)} %get-tuple-element.458, f32[1024]{0:T(1024)S(1)} %get-tuple-element.459, s32[1024]{0:T(1024)S(1)} %fusion.95, s32[128]{0:T(128)S(1)} %iota_add_fusion.4, bf16[1024,576]{1,0:T(8,128)(2,1)} %get-tuple-element.457, s32[]{:T(128)S(6)} %select_n.128), kind=kOutput, calls=%fused_computation.7.clone.clone.1 | convolution fusion | flops 151650304 | bytes 2007556 | tf_op jit(solution)/shard_map/while/body/eval_jaxpr/dot_general | solution.py:23
  50.0 1.4 fusion.97
  51.5 0.7 copy-done.1
  52.1 2.3 %fusion.99 = f32[128,576]{0,1:T(8,128)} fusion(f32[128,576]{0,1:T(8,128)} %get-tuple-element.436, bf16[128,1024]{1,0:T(8,128)(2,1)S(1)} %fusion.97, bf16[1024,576]{1,0:T(8,128)(2,1)S(1)} %copy-done.3, f32[128,512]{0,1:T(8,128)S(1)} %fusion.98), kind=kOutput, calls=%fused_computation.11.clone.clone.1 | convolution fusion | flops 151142400 | bytes 2293760 | tf_op jit(solution)/shard_map/while/body/eval_jaxpr/dot_general | solution.py:54
  54.7 1.8 select_add_fusion.3
  56.5 5.3 %collective-permute-done = f32[128,576]{0,1:T(8,128)} collective-permute-done((f32[128,576]{0,1:T(8,128)}, f32[128,576]{0,1:T(8,128)}, u32[]{:S(2)}, u32[]{:S(2)}) %collective-permute-start) | collective-permute-done | bytes 294944 | tf_op jit(solution)/shard_map/while/body/eval_jaxpr/ppermute | solution.py:13
  61.8 0.6 fusion.95
  62.5 2.0 %fusion.96 = f32[128,1024]{1,0:T(8,128)S(1)} fusion(bf16[1024,576]{1,0:T(8,128)(2,1)} %get-tuple-element.458, f32[1024]{0:T(1024)S(1)} %get-tuple-element.459, s32[1024]{0:T(1024)S(1)} %fusion.95, s32[128]{0:T(128)S(1)} %iota_add_fusion.4, bf16[1024,576]{1,0:T(8,128)(2,1)} %get-tuple-element.457, s32[]{:T(128)S(6)} %select_n.128), kind=kOutput, calls=%fused_computation.7.clone.clone.1 | convolution fusion | flops 151650304 | bytes 2007556 | tf_op jit(solution)/shard_map/while/body/eval_jaxpr/dot_general | solution.py:23
  65.0 1.4 fusion.97
  66.4 0.7 copy-done.1
  67.1 2.3 %fusion.99 = f32[128,576]{0,1:T(8,128)} fusion(f32[128,576]{0,1:T(8,128)} %get-tuple-element.436, bf16[128,1024]{1,0:T(8,128)(2,1)S(1)} %fusion.97, bf16[1024,576]{1,0:T(8,128)(2,1)S(1)} %copy-done.3, f32[128,512]{0,1:T(8,128)S(1)} %fusion.98), kind=kOutput, calls=%fused_computation.11.clone.clone.1 | convolution fusion | flops 151142400 | bytes 2293760 | tf_op jit(solution)/shard_map/while/body/eval_jaxpr/dot_general | solution.py:54
  69.4 1.8 select_add_fusion.3
  71.2 5.6 %collective-permute-done = f32[128,576]{0,1:T(8,128)} collective-permute-done((f32[128,576]{0,1:T(8,128)}, f32[128,576]{0,1:T(8,128)}, u32[]{:S(2)}, u32[]{:S(2)}) %collective-permute-start) | collective-permute-done | bytes 294944 | tf_op jit(solution)/shard_map/while/body/eval_jaxpr/ppermute | solution.py:13
  76.8 0.6 fusion.95
  77.5 2.0 %fusion.96 = f32[128,1024]{1,0:T(8,128)S(1)} fusion(bf16[1024,576]{1,0:T(8,128)(2,1)} %get-tuple-element.458, f32[1024]{0:T(1024)S(1)} %get-tuple-element.459, s32[1024]{0:T(1024)S(1)} %fusion.95, s32[128]{0:T(128)S(1)} %iota_add_fusion.4, bf16[1024,576]{1,0:T(8,128)(2,1)} %get-tuple-element.457, s32[]{:T(128)S(6)} %select_n.128), kind=kOutput, calls=%fused_computation.7.clone.clone.1 | convolution fusion | flops 151650304 | bytes 2007556 | tf_op jit(solution)/shard_map/while/body/eval_jaxpr/dot_general | solution.py:23
  80.0 1.4 fusion.97
  81.4 0.7 copy-done.1
  82.1 2.3 %fusion.99 = f32[128,576]{0,1:T(8,128)} fusion(f32[128,576]{0,1:T(8,128)} %get-tuple-element.436, bf16[128,1024]{1,0:T(8,128)(2,1)S(1)} %fusion.97, bf16[1024,576]{1,0:T(8,128)(2,1)S(1)} %copy-done.3, f32[128,512]{0,1:T(8,128)S(1)} %fusion.98), kind=kOutput, calls=%fused_computation.11.clone.clone.1 | convolution fusion | flops 151142400 | bytes 2293760 | tf_op jit(solution)/shard_map/while/body/eval_jaxpr/dot_general | solution.py:54
  84.4 1.8 select_add_fusion.3
  86.2 5.6 %collective-permute-done = f32[128,576]{0,1:T(8,128)} collective-permute-done((f32[128,576]{0,1:T(8,128)}, f32[128,576]{0,1:T(8,128)}, u32[]{:S(2)}, u32[]{:S(2)}) %collective-permute-start) | collective-permute-done | bytes 294944 | tf_op jit(solution)/shard_map/while/body/eval_jaxpr/ppermute | solution.py:13
  91.8 0.6 fusion.95
  92.4 2.0 %fusion.96 = f32[128,1024]{1,0:T(8,128)S(1)} fusion(bf16[1024,576]{1,0:T(8,128)(2,1)} %get-tuple-element.458, f32[1024]{0:T(1024)S(1)} %get-tuple-element.459, s32[1024]{0:T(1024)S(1)} %fusion.95, s32[128]{0:T(128)S(1)} %iota_add_fusion.4, bf16[1024,576]{1,0:T(8,128)(2,1)} %get-tuple-element.457, s32[]{:T(128)S(6)} %select_n.128), kind=kOutput, calls=%fused_computation.7.clone.clone.1 | convolution fusion | flops 151650304 | bytes 2007556 | tf_op jit(solution)/shard_map/while/body/eval_jaxpr/dot_general | solution.py:23
  95.0 1.4 fusion.97
  96.4 0.7 copy-done.1
  97.1 2.3 %fusion.99 = f32[128,576]{0,1:T(8,128)} fusion(f32[128,576]{0,1:T(8,128)} %get-tuple-element.436, bf16[128,1024]{1,0:T(8,128)(2,1)S(1)} %fusion.97, bf16[1024,576]{1,0:T(8,128)(2,1)S(1)} %copy-done.3, f32[128,512]{0,1:T(8,128)S(1)} %fusion.98), kind=kOutput, calls=%fused_computation.11.clone.clone.1 | convolution fusion | flops 151142400 | bytes 2293760 | tf_op jit(solution)/shard_map/while/body/eval_jaxpr/dot_general | solution.py:54
  99.4 1.8 select_add_fusion.3
  101.2 5.6 %collective-permute-done = f32[128,576]{0,1:T(8,128)} collective-permute-done((f32[128,576]{0,1:T(8,128)}, f32[128,576]{0,1:T(8,128)}, u32[]{:S(2)}, u32[]{:S(2)}) %collective-permute-start) | collective-permute-done | bytes 294944 | tf_op jit(solution)/shard_map/while/body/eval_jaxpr/ppermute | solution.py:13
  106.8 0.6 fusion.95
  107.4 2.0 %fusion.96 = f32[128,1024]{1,0:T(8,128)S(1)} fusion(bf16[1024,576]{1,0:T(8,128)(2,1)} %get-tuple-element.458, f32[1024]{0:T(1024)S(1)} %get-tuple-element.459, s32[1024]{0:T(1024)S(1)} %fusion.95, s32[128]{0:T(128)S(1)} %iota_add_fusion.4, bf16[1024,576]{1,0:T(8,128)(2,1)} %get-tuple-element.457, s32[]{:T(128)S(6)} %select_n.128), kind=kOutput, calls=%fused_computation.7.clone.clone.1 | convolution fusion | flops 151650304 | bytes 2007556 | tf_op jit(solution)/shard_map/while/body/eval_jaxpr/dot_general | solution.py:23
  110.0 1.4 fusion.97
  111.4 0.7 copy-done.1
  112.1 2.3 %fusion.99 = f32[128,576]{0,1:T(8,128)} fusion(f32[128,576]{0,1:T(8,128)} %get-tuple-element.436, bf16[128,1024]{1,0:T(8,128)(2,1)S(1)} %fusion.97, bf16[1024,576]{1,0:T(8,128)(2,1)S(1)} %copy-done.3, f32[128,512]{0,1:T(8,128)S(1)} %fusion.98), kind=kOutput, calls=%fused_computation.11.clone.clone.1 | convolution fusion | flops 151142400 | bytes 2293760 | tf_op jit(solution)/shard_map/while/body/eval_jaxpr/dot_general | solution.py:54
  114.4 1.8 select_add_fusion.3
  116.2 5.6 %collective-permute-done = f32[128,576]{0,1:T(8,128)} collective-permute-done((f32[128,576]{0,1:T(8,128)}, f32[128,576]{0,1:T(8,128)}, u32[]{:S(2)}, u32[]{:S(2)}) %collective-permute-start) | collective-permute-done | bytes 294944 | tf_op jit(solution)/shard_map/while/body/eval_jaxpr/ppermute | solution.py:13
  121.7 0.6 fusion.95
  122.4 2.0 %fusion.96 = f32[128,1024]{1,0:T(8,128)S(1)} fusion(bf16[1024,576]{1,0:T(8,128)(2,1)} %get-tuple-element.458, f32[1024]{0:T(1024)S(1)} %get-tuple-element.459, s32[1024]{0:T(1024)S(1)} %fusion.95, s32[128]{0:T(128)S(1)} %iota_add_fusion.4, bf16[1024,576]{1,0:T(8,128)(2,1)} %get-tuple-element.457, s32[]{:T(128)S(6)} %select_n.128), kind=kOutput, calls=%fused_computation.7.clone.clone.1 | convolution fusion | flops 151650304 | bytes 2007556 | tf_op jit(solution)/shard_map/while/body/eval_jaxpr/dot_general | solution.py:23
  125.0 1.4 fusion.97
  126.4 0.7 copy-done.1
  127.1 2.3 %fusion.99 = f32[128,576]{0,1:T(8,128)} fusion(f32[128,576]{0,1:T(8,128)} %get-tuple-element.436, bf16[128,1024]{1,0:T(8,128)(2,1)S(1)} %fusion.97, bf16[1024,576]{1,0:T(8,128)(2,1)S(1)} %copy-done.3, f32[128,512]{0,1:T(8,128)S(1)} %fusion.98), kind=kOutput, calls=%fused_computation.11.clone.clone.1 | convolution fusion | flops 151142400 | bytes 2293760 | tf_op jit(solution)/shard_map/while/body/eval_jaxpr/dot_general | solution.py:54
  129.4 1.8 select_add_fusion.3
  131.2 5.6 %collective-permute-done = f32[128,576]{0,1:T(8,128)} collective-permute-done((f32[128,576]{0,1:T(8,128)}, f32[128,576]{0,1:T(8,128)}, u32[]{:S(2)}, u32[]{:S(2)}) %collective-permute-start) | collective-permute-done | bytes 294944 | tf_op jit(solution)/shard_map/while/body/eval_jaxpr/ppermute | solution.py:13
  137.4 2.0 %fusion.96 = f32[128,1024]{1,0:T(8,128)S(1)} fusion(bf16[1024,576]{1,0:T(8,128)(2,1)} %get-tuple-element.458, f32[1024]{0:T(1024)S(1)} %get-tuple-element.459, s32[1024]{0:T(1024)S(1)} %fusion.95, s32[128]{0:T(128)S(1)} %iota_add_fusion.4, bf16[1024,576]{1,0:T(8,128)(2,1)} %get-tuple-element.457, s32[]{:T(128)S(6)} %select_n.128), kind=kOutput, calls=%fused_computation.7.clone.clone.1 | convolution fusion | flops 151650304 | bytes 2007556 | tf_op jit(solution)/shard_map/while/body/eval_jaxpr/dot_general | solution.py:23
  139.9 1.4 fusion.97
  141.3 0.7 copy-done.1
  142.0 2.3 %fusion.99 = f32[128,576]{0,1:T(8,128)} fusion(f32[128,576]{0,1:T(8,128)} %get-tuple-element.436, bf16[128,1024]{1,0:T(8,128)(2,1)S(1)} %fusion.97, bf16[1024,576]{1,0:T(8,128)(2,1)S(1)} %copy-done.3, f32[128,512]{0,1:T(8,128)S(1)} %fusion.98), kind=kOutput, calls=%fused_computation.11.clone.clone.1 | convolution fusion | flops 151142400 | bytes 2293760 | tf_op jit(solution)/shard_map/while/body/eval_jaxpr/dot_general | solution.py:54
  144.3 1.8 select_add_fusion.3
  146.1 5.6 %collective-permute-done = f32[128,576]{0,1:T(8,128)} collective-permute-done((f32[128,576]{0,1:T(8,128)}, f32[128,576]{0,1:T(8,128)}, u32[]{:S(2)}, u32[]{:S(2)}) %collective-permute-start) | collective-permute-done | bytes 294944 | tf_op jit(solution)/shard_map/while/body/eval_jaxpr/ppermute | solution.py:13
  151.7 1.9 %copy.14 = f32[128,576]{1,0:T(8,128)} copy(f32[128,576]{0,1:T(8,128)} %get-tuple-element.249) | data formatting | bytes 589824 | tf_op jit(solution)/shard_map/while | solution.py:104
  153.6 1.7 fusion.27
  155.3 0.7 copy-done.5
  156.0 1.1 fusion.28
  157.1 1.5 add_convert_fusion
  158.7 1.4 copy.13
  160.1 17.7 %reduce-scatter.2.cloned.1.call-done = f32[32,576]{1,0:T(8,128)} async-done(((f32[128,576]{1,0:T(8,128)}), f32[32,576]{1,0:T(8,128)}) %reduce-scatter.2.cloned.1.call-update) | async-done | bytes 73744 | tf_op jit(solution)/shard_map/reduce_scatter | solution.py:106
  (69 shorter events, 5.7 us)
Async XLA Ops:
  7.2 30.5 %all-gather.2.cloned.1.call-start = ((), (), s32[]{:S(2)}) async-start(), calls=%async_computation.1 | async-start | bytes 1474560 | tf_op jit(solution)/shard_map/all_gather | solution.py:81
  8.9 168.8 %reduce-scatter.2.cloned.1.call-start = ((), (), s32[]{:S(2)}) async-start(), calls=%async_computation.2 | async-start | bytes 409600 | tf_op jit(solution)/shard_map/reduce_scatter | solution.py:106
  10.9 30.4 %copy-start.9 = (f32[32,32]{1,0:T(8,128)}, f32[32,32]{1,0:T(8,128)S(1)}, u32[]{:S(2)}) copy-start(f32[32,32]{1,0:T(8,128)S(1)} %multiply_reduce_fusion) | copy-start | bytes 12292
  41.3 1.3 copy-start.2
  42.5 2.5 %copy-start = (bf16[32,32,512]{2,1,0:T(8,128)(2,1)S(1)}, bf16[32,32,512]{2,1,0:T(8,128)(2,1)}, u32[]{:S(2)}) copy-start(bf16[32,32,512]{2,1,0:T(8,128)(2,1)} %param.9) | copy-start | bytes 3145732
  44.2 0.8 copy-start.6
  49.5 2.6 %copy-start.3 = (bf16[1024,576]{1,0:T(8,128)(2,1)S(1)}, bf16[1024,576]{1,0:T(8,128)(2,1)}, u32[]{:S(2)}) copy-start(bf16[1024,576]{1,0:T(8,128)(2,1)} %get-tuple-element.458) | copy-start | bytes 3538948 | tf_op jit(solution)/shard_map/while
  51.4 0.7 copy-start.1
  54.4 7.4 %collective-permute-start = (f32[128,576]{0,1:T(8,128)}, f32[128,576]{0,1:T(8,128)}, u32[]{:S(2)}, u32[]{:S(2)}) collective-permute-start(f32[128,576]{0,1:T(8,128)} %fusion.99), channel_id=1, source_target_pairs={{28,0},{0,4},{4,8},{8,12},{12,16},{16,20},{20,24},{24,28},{29,1},{... | collective-permute-start | bytes 884744 | tf_op jit(solution)/shard_map/while/body/eval_jaxpr/ppermute | solution.py:13
  64.5 2.6 %copy-start.3 = (bf16[1024,576]{1,0:T(8,128)(2,1)S(1)}, bf16[1024,576]{1,0:T(8,128)(2,1)}, u32[]{:S(2)}) copy-start(bf16[1024,576]{1,0:T(8,128)(2,1)} %get-tuple-element.458) | copy-start | bytes 3538948 | tf_op jit(solution)/shard_map/while
  66.4 0.7 copy-start.1
  69.4 7.4 %collective-permute-start = (f32[128,576]{0,1:T(8,128)}, f32[128,576]{0,1:T(8,128)}, u32[]{:S(2)}, u32[]{:S(2)}) collective-permute-start(f32[128,576]{0,1:T(8,128)} %fusion.99), channel_id=1, source_target_pairs={{28,0},{0,4},{4,8},{8,12},{12,16},{16,20},{20,24},{24,28},{29,1},{... | collective-permute-start | bytes 884744 | tf_op jit(solution)/shard_map/while/body/eval_jaxpr/ppermute | solution.py:13
  79.5 2.6 %copy-start.3 = (bf16[1024,576]{1,0:T(8,128)(2,1)S(1)}, bf16[1024,576]{1,0:T(8,128)(2,1)}, u32[]{:S(2)}) copy-start(bf16[1024,576]{1,0:T(8,128)(2,1)} %get-tuple-element.458) | copy-start | bytes 3538948 | tf_op jit(solution)/shard_map/while
  81.4 0.7 copy-start.1
  84.4 7.4 %collective-permute-start = (f32[128,576]{0,1:T(8,128)}, f32[128,576]{0,1:T(8,128)}, u32[]{:S(2)}, u32[]{:S(2)}) collective-permute-start(f32[128,576]{0,1:T(8,128)} %fusion.99), channel_id=1, source_target_pairs={{28,0},{0,4},{4,8},{8,12},{12,16},{16,20},{20,24},{24,28},{29,1},{... | collective-permute-start | bytes 884744 | tf_op jit(solution)/shard_map/while/body/eval_jaxpr/ppermute | solution.py:13
  94.5 2.6 %copy-start.3 = (bf16[1024,576]{1,0:T(8,128)(2,1)S(1)}, bf16[1024,576]{1,0:T(8,128)(2,1)}, u32[]{:S(2)}) copy-start(bf16[1024,576]{1,0:T(8,128)(2,1)} %get-tuple-element.458) | copy-start | bytes 3538948 | tf_op jit(solution)/shard_map/while
  96.4 0.7 copy-start.1
  99.4 7.4 %collective-permute-start = (f32[128,576]{0,1:T(8,128)}, f32[128,576]{0,1:T(8,128)}, u32[]{:S(2)}, u32[]{:S(2)}) collective-permute-start(f32[128,576]{0,1:T(8,128)} %fusion.99), channel_id=1, source_target_pairs={{28,0},{0,4},{4,8},{8,12},{12,16},{16,20},{20,24},{24,28},{29,1},{... | collective-permute-start | bytes 884744 | tf_op jit(solution)/shard_map/while/body/eval_jaxpr/ppermute | solution.py:13
  109.4 2.6 %copy-start.3 = (bf16[1024,576]{1,0:T(8,128)(2,1)S(1)}, bf16[1024,576]{1,0:T(8,128)(2,1)}, u32[]{:S(2)}) copy-start(bf16[1024,576]{1,0:T(8,128)(2,1)} %get-tuple-element.458) | copy-start | bytes 3538948 | tf_op jit(solution)/shard_map/while
  111.4 0.7 copy-start.1
  114.4 7.4 %collective-permute-start = (f32[128,576]{0,1:T(8,128)}, f32[128,576]{0,1:T(8,128)}, u32[]{:S(2)}, u32[]{:S(2)}) collective-permute-start(f32[128,576]{0,1:T(8,128)} %fusion.99), channel_id=1, source_target_pairs={{28,0},{0,4},{4,8},{8,12},{12,16},{16,20},{20,24},{24,28},{29,1},{... | collective-permute-start | bytes 884744 | tf_op jit(solution)/shard_map/while/body/eval_jaxpr/ppermute | solution.py:13
  124.4 2.6 %copy-start.3 = (bf16[1024,576]{1,0:T(8,128)(2,1)S(1)}, bf16[1024,576]{1,0:T(8,128)(2,1)}, u32[]{:S(2)}) copy-start(bf16[1024,576]{1,0:T(8,128)(2,1)} %get-tuple-element.458) | copy-start | bytes 3538948 | tf_op jit(solution)/shard_map/while
  126.4 0.7 copy-start.1
  129.3 7.4 %collective-permute-start = (f32[128,576]{0,1:T(8,128)}, f32[128,576]{0,1:T(8,128)}, u32[]{:S(2)}, u32[]{:S(2)}) collective-permute-start(f32[128,576]{0,1:T(8,128)} %fusion.99), channel_id=1, source_target_pairs={{28,0},{0,4},{4,8},{8,12},{12,16},{16,20},{20,24},{24,28},{29,1},{... | collective-permute-start | bytes 884744 | tf_op jit(solution)/shard_map/while/body/eval_jaxpr/ppermute | solution.py:13
  139.4 2.6 %copy-start.3 = (bf16[1024,576]{1,0:T(8,128)(2,1)S(1)}, bf16[1024,576]{1,0:T(8,128)(2,1)}, u32[]{:S(2)}) copy-start(bf16[1024,576]{1,0:T(8,128)(2,1)} %get-tuple-element.458) | copy-start | bytes 3538948 | tf_op jit(solution)/shard_map/while
  141.3 0.7 copy-start.1
  144.3 7.4 %collective-permute-start = (f32[128,576]{0,1:T(8,128)}, f32[128,576]{0,1:T(8,128)}, u32[]{:S(2)}, u32[]{:S(2)}) collective-permute-start(f32[128,576]{0,1:T(8,128)} %fusion.99), channel_id=1, source_target_pairs={{28,0},{0,4},{4,8},{8,12},{12,16},{16,20},{20,24},{24,28},{29,1},{... | collective-permute-start | bytes 884744 | tf_op jit(solution)/shard_map/while/body/eval_jaxpr/ppermute | solution.py:13
  153.6 2.4 %copy-start.4 = (bf16[1024,576]{1,0:T(8,128)(2,1)S(1)}, bf16[1024,576]{1,0:T(8,128)(2,1)}, u32[]{:S(2)}) copy-start(bf16[1024,576]{1,0:T(8,128)(2,1)} %get-tuple-element.474) | copy-start | bytes 3538948
  153.6 2.4 %copy-start.7 = (f32[128,576]{1,0:T(8,128)S(1)}, f32[128,576]{1,0:T(8,128)}, u32[]{:S(2)}) copy-start(f32[128,576]{1,0:T(8,128)} %copy.14) | copy-start | bytes 884740
  153.6 2.4 %copy-start.8 = (f32[128,512]{1,0:T(8,128)S(1)}, f32[128,512]{1,0:T(8,128)}, u32[]{:S(2)}) copy-start(f32[128,512]{1,0:T(8,128)} %fusion.29) | copy-start | bytes 786436
  155.3 0.7 copy-start.5
Sparse Core Ops, SparseCore 0:
  10.4 27.1 all-gather.1
  157.3 20.4 reduce-scatter.1
where the time goes:
time: 186 us; the launch traced here: 185 us
  waiting for transfers between devices  82.3 us (44%)
  matrix products  66.7 us (36%)
  between operations  14.8 us (8%)
  local copies, waits for them, and re-layouts  12.3 us (7%)
  other arithmetic  7.66 us (4%)
    ppermute x7, waiting for transfers between devices, shifted(): return lax.ppermute(block, axis, route)  38.7 us
    all_gather x1, waiting for transfers between devices, per_device(): block_rows = lax.all_gather(latents, 'seq', axis=0, tiled=True)  25.9 us
    dot_general x9, matrix products, score_block(): lax.dot_general(block_rows, query_rows, (((1,), (1,)), ((), ())), preferr...  19.3 us
    reduce_scatter x1, waiting for transfers between devices, per_device(): lax.psum_scatter(owned_sum, 'head', scatter_dimension=0, tiled=True)  17.7 us
    dot_general x8, matrix products, grad_block(): key_term = jnp.dot(dscore, query_rows, preferred_element_type=jnp.float32)  17.2 us
    dot_general x8, matrix products, grad_block(): lax.dot_general(dscore, block_rows, (((0,), (0,)), ((), ())), preferred_e...  14.1 us
    dot_general x8, matrix products, grad_block(): lax.dot_general(block_rows[:, :value_width], grad_rows, (((1,), (1,)), ((...  11.4 us
    while x28, local copies, waits for them, and re-layouts  4.85 us
  transfers between devices with their start and end apart: 9, of which 9 were waited for; matrix products, arithmetic and copies ran while one was open for 9% of the time, Pallas kernels for 0%

commit v1 on v0

v1 whole, which is shorter than its diff:
```python
import functools

import jax
import jax.numpy as jnp
from jax import lax
from jax.experimental import pallas as pl
from jax.experimental.pallas import tpu as pltpu
from jax.sharding import PartitionSpec as P

score_scale = 192 ** (-0.5)
masked_score = -1e30
MESH = pl.DeviceIdType.MESH
NT = (((1,), (1,)), ((), ()))
TN = (((0,), (0,)), ((), ()))


def fused_kernel(
    n_seq, n_head, head_count, tile,
    start_ref, q_hbm, lat_hbm, og_hbm, lo_hbm,
    qgrad_hbm, lgrad_ref,
    q, og, lo, keys, scores, pgrad, w16, ds, delta, run_max, run_sum,
    part, send1, rx1, send2, rx2, own, send3, rx3, qout,
    load_sem, out_sem, ag_send, ag_recv, fw_send, fw_recv,
    s1_send, s1_recv, s2_send, s2_recv, s3_send, s3_recv,
):
    f32, bf16 = jnp.float32, jnp.bfloat16
    me = lax.axis_index("seq")
    my_head = lax.axis_index("head")
    chips = n_seq // 2
    chip, core = me // 2, me % 2
    sibling = chip * 2 + 1 - core
    rows, width = q.shape
    value_width = og.shape[1]
    kb = lat_hbm.shape[0]
    tiles = rows // tile
    piece = kb // n_head

    def peer(step):
        return ((chip + step + chips) % chips) * 2 + core

    loads = [
        pltpu.make_async_copy(lat_hbm, keys.at[pl.ds(0, kb)], load_sem.at[0]),
        pltpu.make_async_copy(q_hbm, q, load_sem.at[1]),
        pltpu.make_async_copy(og_hbm, og, load_sem.at[2]),
        pltpu.make_async_copy(lo_hbm, lo, load_sem.at[3]),
    ]
    for copy in loads:
        copy.start()

    barrier = pltpu.get_barrier_semaphore()
    pl.semaphore_signal(barrier, inc=1, device_id={"seq": sibling}, device_id_type=MESH)
    for step in range(1, chips):
        pl.semaphore_signal(barrier, inc=1, device_id={"seq": peer(step)}, device_id_type=MESH)
    for step in range(1, n_head):
        pl.semaphore_signal(
            barrier, inc=1, device_id={"head": (my_head + step) % n_head}, device_id_type=MESH
        )
    pl.semaphore_wait(barrier, chips + n_head - 1)

    def slot(k, b):
        return keys.at[pl.ds((2 * k + b) * kb, kb)]

    gathers = [None] * chips
    for k in range(1, chips):
        gathers[k] = pltpu.make_async_remote_copy(
            src_ref=lat_hbm, dst_ref=slot(k, 0), send_sem=ag_send.at[k], recv_sem=ag_recv.at[k],
            device_id={"seq": peer(k)}, device_id_type=MESH,
        )
        gathers[k].start()
    relays = [
        pltpu.make_async_remote_copy(
            src_ref=lat_hbm if k == 0 else slot(k, 0), dst_ref=slot(k, 1),
            send_sem=fw_send.at[k], recv_sem=fw_recv.at[k],
            device_id={"seq": sibling}, device_id_type=MESH,
        )
        for k in range(chips)
    ]
    relays[0].start()

    loads[2].wait()
    loads[3].wait()
    ones = jnp.ones((8, value_width), bf16)
    for t in range(tiles):
        at = pl.ds(t * tile, tile)
        product = og[at, :].astype(f32) * lo[at, :].astype(f32)
        high = product.astype(bf16)
        low = (product - high.astype(f32)).astype(bf16)
        total = lax.dot_general(ones, high, NT, preferred_element_type=f32)
        total += lax.dot_general(ones, low, NT, preferred_element_type=f32)
        delta[:, at] = total[0:1, :]
    loads[0].wait()
    loads[1].wait()

    first_query = start_ref[0]
    pair = 2 * kb

    def score_pair(k):
        base = k * pair
        owner = (chip - k + chips) % chips
        row = lax.broadcasted_iota(jnp.int32, (pair, 1), 0)
        second = row // kb
        key_pos = (owner * 2 + (core + second) % 2) * kb + row % kb
        block = keys[pl.ds(base, pair), :]
        for t in range(tiles):
            at = pl.ds(t * tile, tile)
            lane = lax.broadcasted_iota(jnp.int32, (1, tile), 1) + t * tile
            query_pos = first_query + lane // head_count
            s = lax.dot_general(block, q[at, :], NT, preferred_element_type=f32) * score_scale
            s = jnp.where(key_pos <= query_pos, s, masked_score)
            scores[pl.ds(base, pair), at] = s
            top = jnp.max(s, axis=0, keepdims=True)
            if k == 0:
                run_max[:, at] = top
                run_sum[:, at] = jnp.sum(jnp.exp(s - top), axis=0, keepdims=True)
            else:
                before = run_max[:, at]
                top = jnp.maximum(before, top)
                run_max[:, at] = top
                run_sum[:, at] = run_sum[:, at] * jnp.exp(before - top) + jnp.sum(
                    jnp.exp(s - top), axis=0, keepdims=True
                )
            pgrad[pl.ds(base, pair), at] = lax.dot_general(
                block[:, :value_width], og[at, :], NT, preferred_element_type=f32
            )

    for k in range(1, chips):
        gathers[k].wait_recv()
        relays[k].start()
        relays[k - 1].wait_recv()
        score_pair(k - 1)
    relays[chips - 1].wait_recv()
    score_pair(chips - 1)

    run_max[...] = run_max[...] + jnp.log(run_sum[...])

    def grad_pair(k):
        base = k * pair
        for t in range(tiles):
            at = pl.ds(t * tile, tile)
            w = jnp.exp(scores[pl.ds(base, pair), at] - run_max[:, at])
            w16[:, at] = w.astype(bf16)
            ds[pl.ds(base, pair), at] = (
                score_scale * w * (pgrad[pl.ds(base, pair), at] - delta[:, at])
            ).astype(bf16)
        term = jnp.dot(ds[pl.ds(base, pair), :], q[...], preferred_element_type=f32)
        value = jnp.dot(w16[...], og[...], preferred_element_type=f32)
        wide = term[:, :value_width] + value
        tail = term[:, value_width:]
        part[k, :, :value_width] = wide[:kb]
        part[k, :, value_width:] = tail[:kb]
        send1[k, :, :value_width] = wide[kb:].astype(bf16)
        send1[k, :, value_width:] = tail[kb:].astype(bf16)

    pair_sends = [
        pltpu.make_async_remote_copy(
            src_ref=send1.at[k], dst_ref=rx1.at[k], send_sem=s1_send.at[k], recv_sem=s1_recv.at[k],
            device_id={"seq": sibling}, device_id_type=MESH,
        )
        for k in range(chips)
    ]
    chip_sends = [None] + [
        pltpu.make_async_remote_copy(
            src_ref=send2.at[k], dst_ref=rx2.at[k], send_sem=s2_send.at[k], recv_sem=s2_recv.at[k],
            device_id={"seq": peer(-k)}, device_id_type=MESH,
        )
        for k in range(1, chips)
    ]

    def forward(k):
        pair_sends[k].wait_recv()
        send2[k] = (part[k] + rx1[k].astype(f32)).astype(bf16)
        chip_sends[k].start()

    order = list(range(1, chips)) + [0]
    lag = 2
    for n, k in enumerate(order):
        grad_pair(k)
        pair_sends[k].start()
        if n >= lag and order[n - lag] != 0:
            forward(order[n - lag])
    for n in range(max(0, len(order) - lag), len(order)):
        if order[n] != 0:
            forward(order[n])

    for t in range(tiles):
        at = pl.ds(t * tile, tile)
        qout[at, :] = lax.dot_general(
            ds[:, at], keys[...], TN, preferred_element_type=f32
        ).astype(bf16)
    store = pltpu.make_async_copy(qout, qgrad_hbm, out_sem)
    store.start()

    pair_sends[0].wait_recv()
    total = part[0] + rx1[0].astype(f32)
    for k in range(1, chips):
        chip_sends[k].wait_recv()
        total = total + rx2[k].astype(f32)
    for h in range(n_head):
        own[h] = total[h * piece : (h + 1) * piece]
        send3[h] = total[h * piece : (h + 1) * piece].astype(bf16)
    head_sends = [None] * n_head
    for k in range(1, n_head):
        target = (my_head + k) % n_head
        head_sends[k] = pltpu.make_async_remote_copy(
            src_ref=send3.at[target], dst_ref=rx3.at[k],
            send_sem=s3_send.at[k], recv_sem=s3_recv.at[k],
            device_id={"head": target}, device_id_type=MESH,
        )
        head_sends[k].start()
    result = own[my_head]
    for k in range(1, n_head):
        head_sends[k].wait_recv()
        result = result + rx3[k].astype(f32)
    lgrad_ref[...] = result

    for k in range(1, n_head):
        head_sends[k].wait_send()
    for k in range(1, chips):
        gathers[k].wait_send()
        chip_sends[k].wait_send()
    for k in range(chips):
        relays[k].wait_send()
        pair_sends[k].wait_send()
    store.wait()


def per_device(n_seq, n_head, queries, latents, out_grad, layer_out, query_start):
    query_count, head_count, width = queries.shape
    value_width = out_grad.shape[2]
    rows = query_count * head_count
    kb = latents.shape[0]
    total_keys = kb * n_seq
    chips = n_seq // 2
    piece = kb // n_head
    tile = min(256, rows)
    f32, bf16 = jnp.float32, jnp.bfloat16
    anywhere = pl.BlockSpec(memory_space=pl.ANY)
    dma = pltpu.SemaphoreType.DMA
    query_grad, latent_grad = pl.pallas_call(
        functools.partial(fused_kernel, n_seq, n_head, head_count, tile),
        out_shape=(
            jax.ShapeDtypeStruct((rows, width), bf16),
            jax.ShapeDtypeStruct((piece, width), f32),
        ),
        in_specs=[pl.BlockSpec(memory_space=pltpu.SMEM)] + [anywhere] * 4,
        out_specs=(anywhere, pl.BlockSpec(memory_space=pltpu.VMEM)),
        scratch_shapes=[
            pltpu.VMEM((rows, width), bf16),
            pltpu.VMEM((rows, value_width), bf16),
            pltpu.VMEM((rows, value_width), bf16),
            pltpu.VMEM((total_keys, width), bf16),
            pltpu.VMEM((total_keys, rows), f32),
            pltpu.VMEM((total_keys, rows), f32),
            pltpu.VMEM((2 * kb, rows), bf16),
            pltpu.VMEM((total_keys, rows), bf16),
            pltpu.VMEM((1, rows), f32),
            pltpu.VMEM((1, rows), f32),
            pltpu.VMEM((1, rows), f32),
            pltpu.VMEM((chips, kb, width), f32),
            pltpu.VMEM((chips, kb, width), bf16),
            pltpu.VMEM((chips, kb, width), bf16),
            pltpu.VMEM((chips, kb, width), bf16),
            pltpu.VMEM((chips, kb, width), bf16),
            pltpu.VMEM((n_head, piece, width), f32),
            pltpu.VMEM((n_head, piece, width), bf16),
            pltpu.VMEM((n_head, piece, width), bf16),
            pltpu.VMEM((rows, width), bf16),
            dma((4,)), dma(()),
            dma((chips,)), dma((chips,)), dma((chips,)), dma((chips,)),
            dma((chips,)), dma((chips,)), dma((chips,)), dma((chips,)),
            dma((n_head,)), dma((n_head,)),
        ],
        compiler_params=pltpu.CompilerParams(
            collective_id=0, has_side_effects=True, vmem_limit_bytes=56 * 1024 * 1024
        ),
    )(
        query_start,
        queries.reshape(rows, width),
        latents,
        out_grad.reshape(rows, value_width),
        layer_out.reshape(rows, value_width),
    )
    return query_grad.reshape(query_count, head_count, width), latent_grad


def solution(mesh):
    placed = (
        P("seq", "head", None),
        P("seq", None),
        P("seq", "head", None),
        P("seq", "head", None),
        P("seq"),
    )
    return jax.shard_map(
        functools.partial(per_device, mesh.shape["seq"], mesh.shape["head"]),
        mesh=mesh,
        in_specs=placed,
        out_specs=(P("seq", "head", None), P(("seq", "head"), None)),
        check_vma=False,
    )
```

time: 186 us -> 41.9 us (0.23)
  waiting for transfers between devices: 82.3 us -> 0 us
  matrix products: 66.7 us -> 0 us
  Pallas kernels: 0 us -> 35.6 us
  between operations: 14.8 us -> 1.29 us
  other arithmetic: 7.66 us -> 0 us
  local copies, waits for them, and re-layouts: 12.3 us -> 4.87 us
    dot_general x41 -> x0, matrix products: 66.7 us -> none  [the longest x9 19.3 us: score_block(): lax.dot_general(block_rows, query_rows, (((1,), (1,)), ((), ())), preferr...]
    ppermute x7 -> x0, waiting for transfers between devices: 38.7 us -> none  [shifted(): return lax.ppermute(block, axis, route)]
    pallas_call x0 -> x1, Pallas kernels: none -> 35.6 us  [per_device(): pl.pallas_call(functools.partial(fused_kernel, n_seq, n_head, head_count,...]
    all_gather x1 -> x0, waiting for transfers between devices: 25.9 us -> none  [per_device(): block_rows = lax.all_gather(latents, 'seq', axis=0, tiled=True)]
    reduce_scatter x1 -> x0, waiting for transfers between devices: 17.7 us -> none  [per_device(): lax.psum_scatter(owned_sum, 'head', scatter_dimension=0, tiled=True)]
    while x29 -> x0, local copies, waits for them, and re-layouts: 6.71 us -> none
    add x17 -> x0, other arithmetic: 4.58 us -> none  [the longest x8 4.54 us: per_device(): query_pos = query_start[0] + lax.iota(jnp.int32, row_count) // head_count]
    reduce_sum x2 -> x0, other arithmetic: 3.08 us -> none  [the longest x1 1.88 us: per_device(): jnp.sum(out_grad.astype(jnp.float32) * layer_out.astype(jnp.float32), axi...]
  transfers between devices with their start and end apart: 9 -> 0, of which waited for: 9 -> 0; matrix products, arithmetic and copies ran while one was open for 9% -> 0% of each run, Pallas kernels for 0% -> 0%
where the time goes in v1:
time: 41.9 us; the launch traced here: 41.8 us
  Pallas kernels  35.6 us (85%)
  local copies, waits for them, and re-layouts  4.87 us (12%)
  between operations  1.29 us (3%)
    pallas_call x1, Pallas kernels, per_device(): pl.pallas_call(functools.partial(fused_kernel, n_seq, n_head, head_count,...  35.6 us
    unnamed x5, local copies, waits for them, and re-layouts  4.87 us

profile of v1, /device:TPU:0, one launch (start us, length us, event | category | flops | bytes accessed | tf_op | source)
XLA Modules:
  0.0 41.8 jit_solution(14610172669527879552)
XLA Ops:
  1.3 1.7 %copy.7.lat_hbm = bf16[128,576]{1,0:T(8,128)(2,1)} copy(bf16[128,576]{0,1:T(8,128)(2,1)} %param.6) | data formatting | bytes 294912 | tf_op args[1]
  3.0 35.6 %shard_map.68 = (bf16[1024,576]{1,0:T(8,128)(2,1)}, f32[32,576]{1,0:T(8,128)}) custom-call(s32[1]{0:T(128)S(6)} %copy.10.start_ref, bf16[1024,576]{1,0:T(8,128)(2,1)} %bitcast.5, bf16[128,576]{1,0:T(8,128)(2,1)} %copy.7.lat_hbm, bf16[1024,512]{1,0:T(8,128)(2,1)} %bitcast.6, bf16[1024,512]{1,0:T(8,128)(2,1)} %bitcast.7), custom_call_target="tpu_custom_call" | custom-call | tf_op jit(solution)/shard_map/pallas_call | solution.py:239
  38.6 0.0 copy-start
  38.6 2.5 %copy.11 = bf16[32,32,576]{2,1,0:T(8,128)(2,1)} copy(bf16[32,32,576]{2,1,0:T(8,128)(2,1)} %bitcast.4) | data formatting | bytes 2359296
  41.1 0.0 copy-done
  41.1 0.6 %copy.12 = f32[32,576]{1,0:T(8,128)} copy(f32[32,576]{1,0:T(8,128)S(1)} %copy-done) | data formatting | bytes 147456
Async XLA Ops:
  38.6 2.5 %copy-start = (f32[32,576]{1,0:T(8,128)S(1)}, f32[32,576]{1,0:T(8,128)}, u32[]{:S(2)}) copy-start(f32[32,576]{1,0:T(8,128)} %get-tuple-element.9) | copy-start | bytes 221188

commit v2 on v1

--- a/solution.py
+++ b/solution.py
@@ -15,13 +15,14 @@
 
 
 def fused_kernel(
-    n_seq, n_head, head_count, tile,
+    n_seq, n_head, head_count, tile, cut,
     start_ref, q_hbm, lat_hbm, og_hbm, lo_hbm,
-    qgrad_hbm, lgrad_ref,
-    q, og, lo, keys, scores, pgrad, w16, ds, delta, run_max, run_sum,
-    part, send1, rx1, send2, rx2, own, send3, rx3, qout,
-    load_sem, out_sem, ag_send, ag_recv, fw_send, fw_recv,
+    qout, lgrad_ref,
+    q, og, lo, keys_t, keys, scores, pgrad, w16, ds, delta, run_max, run_sum,
+    part, send1, rx1, send2, rx2, own, send3, rx3, own4, send4, rx4, send5, rx5,
+    load_sem, ag_send, ag_recv, fw_send, fw_recv,
     s1_send, s1_recv, s2_send, s2_recv, s3_send, s3_recv,
+    s4_send, s4_recv, s5_send, s5_recv,
 ):
     f32, bf16 = jnp.float32, jnp.bfloat16
     me = lax.axis_index("seq")
@@ -31,15 +32,22 @@
     sibling = chip * 2 + 1 - core
     rows, width = q.shape
     value_width = og.shape[1]
-    kb = lat_hbm.shape[0]
+    kb = lat_hbm.shape[1]
     tiles = rows // tile
     piece = kb // n_head
 
-    def peer(step):
-        return ((chip + step + chips) % chips) * 2 + core
+    def other_chip(k):
+        found = 0
+        for bit in range(chips.bit_length() - 1):
+            size = 2**bit
+            found += (chip // size % 2 + k // size % 2) % 2 * size
+        return found
+
+    def peer(k):
+        return other_chip(k) * 2 + core
 
     loads = [
-        pltpu.make_async_copy(lat_hbm, keys.at[pl.ds(0, kb)], load_sem.at[0]),
+        pltpu.make_async_copy(lat_hbm, keys_t.at[0], load_sem.at[0]),
         pltpu.make_async_copy(q_hbm, q, load_sem.at[1]),
         pltpu.make_async_copy(og_hbm, og, load_sem.at[2]),
         pltpu.make_async_copy(lo_hbm, lo, load_sem.at[3]),
@@ -58,15 +66,35 @@
     pl.semaphore_wait(barrier, chips + n_head - 1)
 
     def slot(k, b):
-        return keys.at[pl.ds((2 * k + b) * kb, kb)]
-
-    gathers = [None] * chips
-    for k in range(1, chips):
-        gathers[k] = pltpu.make_async_remote_copy(
-            src_ref=lat_hbm, dst_ref=slot(k, 0), send_sem=ag_send.at[k], recv_sem=ag_recv.at[k],
+        return keys_t.at[2 * k + b]
+
+    side = my_head % 2
+    partner = my_head + 1 - 2 * side
+    quarter = width // 4
+    outer = pl.ds(pl.multiple_of(side * 3 * quarter, quarter), quarter)
+    middle = pl.ds(quarter, 2 * quarter)
+
+    def gather(k, part_rows, index):
+        return pltpu.make_async_remote_copy(
+            src_ref=lat_hbm.at[part_rows, :], dst_ref=keys_t.at[2 * k, part_rows, :],
+            send_sem=ag_send.at[k, index], recv_sem=ag_recv.at[k, index],
             device_id={"seq": peer(k)}, device_id_type=MESH,
         )
-        gathers[k].start()
+
+    outer_gathers = [None] + [gather(k, outer, 0) for k in range(1, chips)]
+    middle_gathers = [None] + [gather(k, middle, 1) for k in range(1, chips)]
+    swaps = [None] + [
+        pltpu.make_async_remote_copy(
+            src_ref=keys_t.at[2 * k, outer, :], dst_ref=keys_t.at[2 * k, outer, :],
+            send_sem=ag_send.at[k, 2], recv_sem=ag_recv.at[k, 2],
+            device_id={"head": partner}, device_id_type=MESH,
+        )
+        for k in range(1, chips)
+    ]
+    for k in range(1, chips):
+        outer_gathers[k].start()
+    for k in range(1, chips):
+        middle_gathers[k].start()
     relays = [
         pltpu.make_async_remote_copy(
             src_ref=lat_hbm if k == 0 else slot(k, 0), dst_ref=slot(k, 1),
@@ -88,6 +116,9 @@
         total = lax.dot_general(ones, high, NT, preferred_element_type=f32)
         total += lax.dot_general(ones, low, NT, preferred_element_type=f32)
         delta[:, at] = total[0:1, :]
+    for k in range(1, chips):
+        outer_gathers[k].wait_recv()
+        swaps[k].start()
     loads[0].wait()
     loads[1].wait()
 
@@ -96,10 +127,12 @@
 
     def score_pair(k):
         base = k * pair
-        owner = (chip - k + chips) % chips
+        owner = other_chip(k)
         row = lax.broadcasted_iota(jnp.int32, (pair, 1), 0)
         second = row // kb
         key_pos = (owner * 2 + (core + second) % 2) * kb + row % kb
+        for b in range(2):
+            keys[pl.ds(base + b * kb, kb), :] = keys_t[2 * k + b].T
         block = keys[pl.ds(base, pair), :]
         for t in range(tiles):
             at = pl.ds(t * tile, tile)
@@ -123,9 +156,16 @@
                 block[:, :value_width], og[at, :], NT, preferred_element_type=f32
             )
 
-    for k in range(1, chips):
-        gathers[k].wait_recv()
+    def arrived(k):
+        middle_gathers[k].wait_recv()
+        swaps[k].wait_recv()
         relays[k].start()
+
+    relays[0].wait_recv()
+    score_pair(0)
+    arrived(1)
+    for k in range(2, chips):
+        arrived(k)
         relays[k - 1].wait_recv()
         score_pair(k - 1)
     relays[chips - 1].wait_recv()
@@ -151,6 +191,19 @@
         send1[k, :, :value_width] = wide[kb:].astype(bf16)
         send1[k, :, value_width:] = tail[kb:].astype(bf16)
 
+    def pack(wide):
+        body = wide[:, : value_width - cut]
+        tail = wide[:, value_width - cut :]
+        half = piece // 2
+        lanes = jnp.concatenate([tail[:half], tail[half:]], axis=1)
+        return jnp.concatenate([body, lanes], axis=0)
+
+    def chip_copy(src, dst, send_sem, recv_sem, k):
+        return pltpu.make_async_remote_copy(
+            src_ref=src.at[k], dst_ref=dst.at[k], send_sem=send_sem.at[k], recv_sem=recv_sem.at[k],
+            device_id={"seq": peer(k)}, device_id_type=MESH,
+        )
+
     pair_sends = [
         pltpu.make_async_remote_copy(
             src_ref=send1.at[k], dst_ref=rx1.at[k], send_sem=s1_send.at[k], recv_sem=s1_recv.at[k],
@@ -159,39 +212,69 @@
         for k in range(chips)
     ]
     chip_sends = [None] + [
-        pltpu.make_async_remote_copy(
-            src_ref=send2.at[k], dst_ref=rx2.at[k], send_sem=s2_send.at[k], recv_sem=s2_recv.at[k],
-            device_id={"seq": peer(-k)}, device_id_type=MESH,
-        )
-        for k in range(1, chips)
-    ]
+        chip_copy(send2, rx2, s2_send, s2_recv, k) for k in range(1, chips)
+    ]
+    late_chip_sends = [None] + [
+        chip_copy(send5, rx5, s5_send, s5_recv, k) for k in range(1, chips)
+    ]
+    early_head_sends = [[None] * n_head for _ in range(chips)]
+    for k in range(chips):
+        for d in range(1, n_head):
+            target = (my_head + d) % n_head
+            early_head_sends[k][d] = pltpu.make_async_remote_copy(
+                src_ref=send4.at[k, target], dst_ref=rx4.at[k, d],
+                send_sem=s4_send.at[k, d], recv_sem=s4_recv.at[k, d],
+                device_id={"head": target}, device_id_type=MESH,
+            )
 
     def forward(k):
         pair_sends[k].wait_recv()
-        send2[k] = (part[k] + rx1[k].astype(f32)).astype(bf16)
-        chip_sends[k].start()
-
-    order = list(range(1, chips)) + [0]
-    lag = 2
-    for n, k in enumerate(order):
-        grad_pair(k)
-        pair_sends[k].start()
-        if n >= lag and order[n - lag] != 0:
-            forward(order[n - lag])
-    for n in range(max(0, len(order) - lag), len(order)):
-        if order[n] != 0:
-            forward(order[n])
-
-    for t in range(tiles):
+        total = part[k] + rx1[k].astype(f32)
+        if k:
+            send2[k] = total[:, :cut].astype(bf16)
+            chip_sends[k].start()
+        else:
+            part[0, :, :cut] = total[:, :cut]
+        for h in range(n_head):
+            packed = pack(total[h * piece : (h + 1) * piece, cut:])
+            own4[k, h] = packed
+            send4[k, h] = packed.astype(bf16)
+        for d in range(1, n_head):
+            early_head_sends[k][d].start()
+
+    def query_tile(t):
         at = pl.ds(t * tile, tile)
         qout[at, :] = lax.dot_general(
             ds[:, at], keys[...], TN, preferred_element_type=f32
         ).astype(bf16)
-    store = pltpu.make_async_copy(qout, qgrad_hbm, out_sem)
-    store.start()
-
-    pair_sends[0].wait_recv()
-    total = part[0] + rx1[0].astype(f32)
+
+    order = list(range(chips - 1, -1, -1))
+    lag = 1
+    for n, k in enumerate(order):
+        grad_pair(k)
+        pair_sends[k].start()
+        if n >= lag:
+            forward(order[n - lag])
+    for n in range(max(0, len(order) - lag), len(order)):
+        forward(order[n])
+
+    before = (tiles + 1) // 2
+    for t in range(before):
+        query_tile(t)
+
+    late = None
+    for k in order:
+        total = own4[k, my_head]
+        for d in range(1, n_head):
+            early_head_sends[k][d].wait_recv()
+            total = total + rx4[k, d].astype(f32)
+        if k:
+            send5[k] = total.astype(bf16)
+            late_chip_sends[k].start()
+        else:
+            late = total
+
+    total = part[0, :, :cut]
     for k in range(1, chips):
         chip_sends[k].wait_recv()
         total = total + rx2[k].astype(f32)
@@ -199,29 +282,45 @@
         own[h] = total[h * piece : (h + 1) * piece]
         send3[h] = total[h * piece : (h + 1) * piece].astype(bf16)
     head_sends = [None] * n_head
-    for k in range(1, n_head):
-        target = (my_head + k) % n_head
-        head_sends[k] = pltpu.make_async_remote_copy(
-            src_ref=send3.at[target], dst_ref=rx3.at[k],
-            send_sem=s3_send.at[k], recv_sem=s3_recv.at[k],
+    for d in range(1, n_head):
+        target = (my_head + d) % n_head
+        head_sends[d] = pltpu.make_async_remote_copy(
+            src_ref=send3.at[target], dst_ref=rx3.at[d],
+            send_sem=s3_send.at[d], recv_sem=s3_recv.at[d],
             device_id={"head": target}, device_id_type=MESH,
         )
-        head_sends[k].start()
+        head_sends[d].start()
+
+    for t in range(before, tiles):
+        query_tile(t)
+
+    for k in range(1, chips):
+        late_chip_sends[k].wait_recv()
+        late = late + rx5[k].astype(f32)
+    half = piece // 2
+    lgrad_ref[:, cut:value_width] = late[:piece]
+    lgrad_ref[:half, value_width:] = late[piece:, : width - value_width]
+    lgrad_ref[half:, value_width:] = late[piece:, width - value_width :]
+
     result = own[my_head]
-    for k in range(1, n_head):
-        head_sends[k].wait_recv()
-        result = result + rx3[k].astype(f32)
-    lgrad_ref[...] = result
-
-    for k in range(1, n_head):
-        head_sends[k].wait_send()
-    for k in range(1, chips):
-        gathers[k].wait_send()
+    for d in range(1, n_head):
+        head_sends[d].wait_recv()
+        result = result + rx3[d].astype(f32)
+    lgrad_ref[:, :cut] = result
+
+    for d in range(1, n_head):
+        head_sends[d].wait_send()
+    for k in range(1, chips):
+        outer_gathers[k].wait_send()
+        middle_gathers[k].wait_send()
+        swaps[k].wait_send()
         chip_sends[k].wait_send()
+        late_chip_sends[k].wait_send()
     for k in range(chips):
         relays[k].wait_send()
         pair_sends[k].wait_send()
-    store.wait()
+        for d in range(1, n_head):
+            early_head_sends[k][d].wait_send()
 
 
 def per_device(n_seq, n_head, queries, latents, out_grad, layer_out, query_start):
@@ -233,21 +332,24 @@
     chips = n_seq // 2
     piece = kb // n_head
     tile = min(256, rows)
+    cut = value_width - 128
+    packed = piece + piece * (width - value_width) // 128
     f32, bf16 = jnp.float32, jnp.bfloat16
     anywhere = pl.BlockSpec(memory_space=pl.ANY)
     dma = pltpu.SemaphoreType.DMA
     query_grad, latent_grad = pl.pallas_call(
-        functools.partial(fused_kernel, n_seq, n_head, head_count, tile),
+        functools.partial(fused_kernel, n_seq, n_head, head_count, tile, cut),
         out_shape=(
-            jax.ShapeDtypeStruct((rows, width), bf16),
-            jax.ShapeDtypeStruct((piece, width), f32),
+            pltpu.VMEM((rows, width), bf16),
+            pltpu.VMEM((piece, width), f32),
         ),
         in_specs=[pl.BlockSpec(memory_space=pltpu.SMEM)] + [anywhere] * 4,
-        out_specs=(anywhere, pl.BlockSpec(memory_space=pltpu.VMEM)),
+        out_specs=(pl.BlockSpec(memory_space=pltpu.VMEM),) * 2,
         scratch_shapes=[
             pltpu.VMEM((rows, width), bf16),
             pltpu.VMEM((rows, value_width), bf16),
             pltpu.VMEM((rows, value_width), bf16),
+            pltpu.VMEM((2 * chips, width, kb), bf16),
             pltpu.VMEM((total_keys, width), bf16),
             pltpu.VMEM((total_keys, rows), f32),
             pltpu.VMEM((total_keys, rows), f32),
@@ -259,16 +361,21 @@
             pltpu.VMEM((chips, kb, width), f32),
             pltpu.VMEM((chips, kb, width), bf16),
             pltpu.VMEM((chips, kb, width), bf16),
-            pltpu.VMEM((chips, kb, width), bf16),
-            pltpu.VMEM((chips, kb, width), bf16),
-            pltpu.VMEM((n_head, piece, width), f32),
-            pltpu.VMEM((n_head, piece, width), bf16),
-            pltpu.VMEM((n_head, piece, width), bf16),
-            pltpu.VMEM((rows, width), bf16),
-            dma((4,)), dma(()),
-            dma((chips,)), dma((chips,)), dma((chips,)), dma((chips,)),
+            pltpu.VMEM((chips, kb, cut), bf16),
+            pltpu.VMEM((chips, kb, cut), bf16),
+            pltpu.VMEM((n_head, piece, cut), f32),
+            pltpu.VMEM((n_head, piece, cut), bf16),
+            pltpu.VMEM((n_head, piece, cut), bf16),
+            pltpu.VMEM((chips, n_head, packed, 128), f32),
+            pltpu.VMEM((chips, n_head, packed, 128), bf16),
+            pltpu.VMEM((chips, n_head, packed, 128), bf16),
+            pltpu.VMEM((chips, packed, 128), bf16),
+            pltpu.VMEM((chips, packed, 128), bf16),
+            dma((4,)),
+            dma((chips, 3)), dma((chips, 3)), dma((chips,)), dma((chips,)),
             dma((chips,)), dma((chips,)), dma((chips,)), dma((chips,)),
             dma((n_head,)), dma((n_head,)),
+            dma((chips, n_head)), dma((chips, n_head)), dma((chips,)), dma((chips,)),
         ],
         compiler_params=pltpu.CompilerParams(
             collective_id=0, has_side_effects=True, vmem_limit_bytes=56 * 1024 * 1024
@@ -276,7 +383,7 @@
     )(
         query_start,
         queries.reshape(rows, width),
-        latents,
+        latents.T,
         out_grad.reshape(rows, value_width),
         layer_out.reshape(rows, value_width),
     )

time: 41.9 us -> 33.3 us (0.79)
  Pallas kernels: 35.6 us -> 30.2 us
  local copies, waits for them, and re-layouts: 4.87 us -> 1.69 us
    pallas_call x1, Pallas kernels: 35.6 us -> 30.2 us  [per_device(): pl.pallas_call(functools.partial(fused_kernel, n_seq, n_head, head_count,...]
    unnamed x5 -> x2, local copies, waits for them, and re-layouts: 4.87 us -> 1.69 us
where the time goes in v2:
time: 33.3 us; the launch traced here: 33.2 us
  Pallas kernels  30.2 us (91%)
  local copies, waits for them, and re-layouts  1.69 us (5%)
  between operations  1.29 us (4%)
    pallas_call x1, Pallas kernels, per_device(): pl.pallas_call(functools.partial(fused_kernel, n_seq, n_head, head_count,...  30.2 us
    unnamed x2, local copies, waits for them, and re-layouts  1.69 us

profile of v2, /device:TPU:0, one launch (start us, length us, event | category | flops | bytes accessed | tf_op | source)
XLA Modules:
  0.0 33.2 jit_solution(5448398145754101084)
XLA Ops:
  1.3 30.2 %shard_map.68 = (bf16[1024,576]{1,0:T(8,128)(2,1)S(1)}, f32[32,576]{1,0:T(8,128)S(1)}) custom-call(s32[1]{0:T(128)S(6)} %copy.11.start_ref, bf16[1024,576]{1,0:T(8,128)(2,1)} %bitcast.6, bf16[576,128]{1,0:T(8,128)(2,1)} %bitcast.9, bf16[1024,512]{1,0:T(8,128)(2,1)} %bitcast.7, bf16[1024,512]{1,0:T(8,128)(2,1)} %bitcast.8), custom_call_target="tpu_custom_call" | custom-call | tf_op jit(solution)/shard_map/pallas_call | solution.py:340
  31.5 1.1 %copy.9 = bf16[32,32,576]{2,1,0:T(8,128)(2,1)} copy(bf16[32,32,576]{2,1,0:T(8,128)(2,1)S(1)} %bitcast.5) | data formatting | bytes 2359296
  32.5 0.6 %copy.10 = f32[32,576]{1,0:T(8,128)} copy(f32[32,576]{1,0:T(8,128)S(1)} %get-tuple-element.7) | data formatting | bytes 147456
